TPU v7x, 32 devices: a whole 2x2x4 slice. The times are simulated.
32 devices in a mesh: groups: 2 (over x), wide: 8 (over z, y), narrow: 2 (over core).
Axes of the slice: x: 2, y: 2, z: 4, core: 2. Of those that a mesh axis runs over, the one named last changes fastest.
Arguments:
- context_symbol_ids: int32 [2, 16, 16], P('narrow', 'groups'), parts along dimension 1, may hold values from 0 to 32767
- context_symbol_spans: int32 [2, 16], P('narrow', 'groups'), parts along dimension 1, may hold values from 1 to 16, as said below
- symbol_vector_lookup: bfloat16 [4096, 32768], P('wide'), may hold values from -6 to 6
- opening_lagged_blend: float32 [4096], replicated, may hold values from 0 to 1
- lagged_blend_weights: float32 [3, 4096], replicated, may hold values from 0 to 1
- blending_left_operand: bfloat16 [4096, 192], replicated, may hold values from -0.09375 to 0.09375
- blending_right_operands: bfloat16 [3, 64, 4096], replicated, may hold values from -0.375 to 0.375
- fixed_fading_scores: float32 [4096], P('wide'), may hold values from -6 to -1
- fading_left_operand: bfloat16 [4096, 128], replicated, may hold values from -0.09375 to 0.09375
- fading_right_operand: bfloat16 [128, 4096], P(None, 'wide'), may hold values from -0.5 to 0.5
- address_projector: bfloat16 [4096, 4096], P('wide'), may hold values from -0.09375 to 0.09375
- payload_projector: bfloat16 [4096, 4096], P('wide'), may hold values from -0.09375 to 0.09375
- present_symbol_reward: float32 [64, 64], replicated, may hold values from -1 to 1
- cluster_scaling_weight: float32 [4096], replicated, may hold values from 0.5 to 1.5
- cluster_scaling_offset: float32 [4096], replicated, may hold values from -3 to 3
- generated_acceptance: bfloat16 [2, 16, 4, 4096], P(None, ('groups', 'wide'), None, 'narrow'), parts along dimension 1, may hold values from -6 to 6
- generated_addresses: bfloat16 [2, 16, 4, 4096], P(None, ('groups', 'wide'), None, 'narrow'), parts along dimension 1, may hold values from -6 to 6
- generated_payloads: bfloat16 [2, 16, 4, 4096], P(None, ('groups', 'wide'), None, 'narrow'), parts along dimension 1, may hold values from -6 to 6
- generated_fading_scores: bfloat16 [2, 16, 4, 4096], P(None, ('groups', 'wide'), None, 'narrow'), parts along dimension 1, may hold values from -6 to -1
- generated_valve_scores: bfloat16 [2, 16, 4, 4096], P(None, ('groups', 'wide'), None, 'narrow'), parts along dimension 1, may hold values from -6 to 6
Outputs:
- dec_out: bfloat16 [2, 16, 4, 4096], P(None, ('groups', 'wide'), None, 'narrow'), parts along dimension 1
There are 2 independent parts, one for each index of `groups`. A program takes and returns all parts, laid end to end along the dimension named above; an argument that names none is the same for every part. Nothing has to cross between parts.
Inputs may be any that keep to these rules, and one draw needn't show every extreme that they name: `context_symbol_spans`: positions at or past a prompt's length are padding. In every draw one of the 2 banks, chosen by the draw, holds only prompts of exactly 16 tokens, and every other bank holds at least one prompt of 16 tokens.
All inputs are finite; a program needn't handle non-finite values.
Results may differ from a plain program's by a relative error of at most 0.0095.
Values may be sent and summed in bfloat16 or wider, within the bound.
No kernel may reach another device: no remote copies, remote signals or barrier semaphores. Data moves between devices by JAX's collectives and lax.ppermute only.
A program may use at most 128 MiB of HBM per device.

v0:
```python
import jax
import jax.numpy as jnp
from jax import lax
from jax.sharding import PartitionSpec as P

norm_eps = 0.00064


def mix_project(
    embedded,
    opening_lagged_blend,
    lagged_blend_weights,
    blending_left_operand,
    blending_right_operands,
    fixed_fading_scores,
    fading_left_operand,
    fading_right_operand,
    address_projector,
    payload_projector,
):
    features = embedded.shape[2]
    previous = jnp.pad(embedded, ((0, 0), (1, 0), (0, 0)))[:, :-1, :]
    current = embedded.reshape(-1, features).astype(jnp.float32)
    difference = previous.reshape(-1, features).astype(jnp.float32) - current
    mixed_in = (current + difference * opening_lagged_blend).astype(jnp.bfloat16)
    hidden = jnp.tanh(
        jnp.dot(mixed_in, blending_left_operand, preferred_element_type=jnp.float32)
    ).astype(jnp.bfloat16)
    rank_size = blending_right_operands.shape[1]
    branches = []
    for branch in range(3):
        shift_term = jnp.dot(
            hidden[:, branch * rank_size : (branch + 1) * rank_size],
            blending_right_operands[branch],
            preferred_element_type=jnp.float32,
        )
        branches.append(
            (current + difference * (lagged_blend_weights[branch] + shift_term)).astype(
                jnp.bfloat16
            )
        )
    decay_hidden = jnp.tanh(
        jnp.dot(branches[0], fading_left_operand, preferred_element_type=jnp.float32)
    ).astype(jnp.bfloat16)
    decay_log = fixed_fading_scores + jnp.dot(
        decay_hidden, fading_right_operand, preferred_element_type=jnp.float32
    )
    key_proj = jnp.dot(branches[1], address_projector.T, preferred_element_type=jnp.float32).astype(
        jnp.bfloat16
    )
    value_proj = jnp.dot(
        branches[2], payload_projector.T, preferred_element_type=jnp.float32
    ).astype(jnp.bfloat16)
    return (key_proj, value_proj, decay_log)


def final_states(key_proj, value_proj, decay_log, lengths, attender_width):
    bank_rows, length, columns = key_proj.shape
    attender_ordinal = columns // attender_width
    decay_rates = jnp.exp(decay_log)
    places = lax.broadcasted_iota(jnp.int32, (bank_rows, length), 1)
    live_mask = (places < lengths[:, None])[:, :, None]
    running = jnp.cumsum(jnp.where(live_mask, decay_rates, 0.0), axis=1)
    remaining = running[:, -1:, :] - running
    weights = jnp.where(live_mask, jnp.exp(-remaining), 0.0)
    weighted = (key_proj.astype(jnp.float32) * weights).reshape(
        bank_rows, length, attender_ordinal, attender_width
    )
    plain_values = value_proj.astype(jnp.float32).reshape(
        bank_rows, length, attender_ordinal, attender_width
    )
    return jnp.einsum("rlhi,rlhj->rhij", weighted, plain_values, precision=lax.Precision.HIGHEST)


def generation_iterations(
    recurrent_memories,
    acceptance_lines,
    address_source,
    payload_source,
    fading_source,
    valve_source,
    shard_reward,
    shard_scaling_weight,
    shard_scaling_offset,
):
    attender_ordinal = recurrent_memories.shape[-3]
    attender_width = recurrent_memories.shape[-1]
    leading = acceptance_lines.shape[:-2]
    step_count = acceptance_lines.shape[-2]
    split_shape = leading + (step_count, attender_ordinal, attender_width)
    receptance = acceptance_lines.astype(jnp.float32).reshape(split_shape)
    key_split = address_source.astype(jnp.float32).reshape(split_shape)
    valued = payload_source.astype(jnp.float32).reshape(split_shape)
    factors = jnp.exp(-jnp.exp(fading_source.astype(jnp.float32))).reshape(split_shape)
    results = []
    for position in range(step_count):
        present_acceptance = receptance[..., position, :, :]
        present_address = key_split[..., position, :, :]
        present_payload = valued[..., position, :, :]
        immediate_summand = (
            jnp.sum(present_acceptance * shard_reward * present_address, axis=-1, keepdims=True)
            * present_payload
        )
        carried = jnp.einsum(
            "...hi,...hij->...hj",
            present_acceptance,
            recurrent_memories,
            precision=lax.Precision.HIGHEST,
        )
        results.append(carried + immediate_summand)
        if position + 1 < step_count:
            recurrent_memories = (
                factors[..., position, :, :][..., :, None] * recurrent_memories
                + present_address[..., :, None] * present_payload[..., None, :]
            )
    mixed_out = jnp.stack(results, axis=-3)
    average = jnp.mean(mixed_out, axis=-1, keepdims=True)
    centred = mixed_out - average
    spread = jnp.mean(centred * centred, axis=-1, keepdims=True)
    normed = (centred * lax.rsqrt(spread + norm_eps)).reshape(
        leading + (step_count, attender_ordinal * attender_width)
    )
    return (
        (normed * shard_scaling_weight + shard_scaling_offset)
        * jax.nn.silu(valve_source.astype(jnp.float32))
    ).astype(jnp.bfloat16)


def per_device(
    context_symbol_ids,
    context_symbol_spans,
    symbol_vector_lookup,
    opening_lagged_blend,
    lagged_blend_weights,
    blending_left_operand,
    blending_right_operands,
    fixed_fading_scores,
    fading_left_operand,
    fading_right_operand,
    address_projector,
    payload_projector,
    present_symbol_reward,
    cluster_scaling_weight,
    cluster_scaling_offset,
    generated_acceptance,
    generated_addresses,
    generated_payloads,
    generated_fading_scores,
    generated_valve_scores,
):
    bank_rows = context_symbol_ids.shape[1]
    length = context_symbol_ids.shape[2]
    columns = symbol_vector_lookup.shape[0]
    attender_width = present_symbol_reward.shape[1]
    head_local = columns // attender_width
    lengths = context_symbol_spans.reshape(-1)
    picked = jnp.take(symbol_vector_lookup, context_symbol_ids.reshape(-1), axis=1)
    gathered = lax.all_gather(picked, "wide", axis=0, tiled=True).T
    features = gathered.shape[1]
    block_rows = bank_rows
    while block_rows % 2 == 0 and block_rows * length > 1024:
        block_rows = block_rows // 2
    blocks = gathered.reshape(bank_rows // block_rows, block_rows, length, features)
    length_blocks = lengths.reshape(bank_rows // block_rows, block_rows)

    def one_block(block_item):
        key_proj, value_proj, decay_log = mix_project(
            block_item[0],
            opening_lagged_blend,
            lagged_blend_weights,
            blending_left_operand,
            blending_right_operands,
            fixed_fading_scores,
            fading_left_operand,
            fading_right_operand,
            address_projector,
            payload_projector,
        )
        block_shape = (block_rows, length, columns)
        return final_states(
            key_proj.reshape(block_shape),
            value_proj.reshape(block_shape),
            decay_log.reshape(block_shape),
            block_item[1],
            attender_width,
        )

    recurrent_memories = lax.map(one_block, (blocks, length_blocks)).reshape(
        bank_rows, head_local, attender_width, attender_width
    )
    handed = lax.all_to_all(
        lax.all_to_all(
            recurrent_memories.reshape(1, bank_rows, head_local, attender_width * attender_width),
            "wide",
            split_axis=1,
            concat_axis=2,
            tiled=True,
        ),
        "narrow",
        split_axis=2,
        concat_axis=0,
        tiled=True,
    )
    generated_by_attender = handed.shape[2]
    leading_attender_offset = lax.axis_index("narrow") * generated_by_attender
    shard_reward = lax.dynamic_slice_in_dim(
        present_symbol_reward, leading_attender_offset, generated_by_attender, 0
    )
    shard_scaling_weight = lax.dynamic_slice_in_dim(
        cluster_scaling_weight,
        leading_attender_offset * attender_width,
        generated_by_attender * attender_width,
        0,
    )
    shard_scaling_offset = lax.dynamic_slice_in_dim(
        cluster_scaling_offset,
        leading_attender_offset * attender_width,
        generated_by_attender * attender_width,
        0,
    )
    result = generation_iterations(
        handed.reshape(handed.shape[:3] + (attender_width, attender_width)),
        generated_acceptance,
        generated_addresses,
        generated_payloads,
        generated_fading_scores,
        generated_valve_scores,
        shard_reward,
        shard_scaling_weight,
        shard_scaling_offset,
    )
    return result


def solution(mesh):
    placed = (
        P("narrow", "groups", None),
        P("narrow", "groups"),
        P("wide", None),
        P(),
        P(),
        P(),
        P(),
        P("wide"),
        P(),
        P(None, "wide"),
        P("wide", None),
        P("wide", None),
        P(),
        P(),
        P(),
        P(None, ("groups", "wide"), None, "narrow"),
        P(None, ("groups", "wide"), None, "narrow"),
        P(None, ("groups", "wide"), None, "narrow"),
        P(None, ("groups", "wide"), None, "narrow"),
        P(None, ("groups", "wide"), None, "narrow"),
    )
    return jax.shard_map(
        per_device,
        mesh=mesh,
        in_specs=placed,
        out_specs=P(None, ("groups", "wide"), None, "narrow"),
        check_vma=False,
    )
```

profile of v0, /device:TPU:0, one launch (start us, length us, event | category | flops | bytes accessed | tf_op | source)
XLA Modules:
  0.0 180.6 jit_solution(2919527989202924769)
XLA Ops:
  6.5 0.9 reshape.534
  7.4 0.8 reshape.533
  8.2 44.0 %copy.70 = bf16[512,32768]{0,1:T(8,128)(2,1)} copy(bf16[512,32768]{1,0:T(8,128)(2,1)} %param.22) | data formatting | bytes 67108864 | tf_op args[2]
  52.2 2.0 %gather_fusion = bf16[128,512]{1,0:T(8,128)(2,1)S(1)} fusion(bf16[512,32768]{0,1:T(8,128)(2,1)} %copy.70, s32[1024]{0:T(1024)S(1)} %pad_clamp_fusion), kind=kCustom, calls=%fused_computation | custom fusion | bytes 262656 | tf_op jit(solution)/shard_map/jit(_take)/gather | solution.py:157
  54.2 0.7 select_bitcast_fusion
  55.1 42.1 %all-gather.2.cloned.1.call-done = bf16[4096,128]{0,1:T(8,128)(2,1)} async-done(((bf16[512,128]{0,1:T(8,128)(2,1)}), bf16[4096,128]{0,1:T(8,128)(2,1)}) %all-gather.2.cloned.1.call-update) | async-done | bytes 1048592 | tf_op jit(solution)/shard_map/all_gather | solution.py:158
  97.2 1.6 pad_slice_fusion
  98.8 0.7 fusion.20
  99.8 2.7 %fusion.22 = bf16[128,128]{1,0:T(8,128)(2,1)S(1)} fusion(bf16[4096,128]{1,0:T(8,128)(2,1)} %param.28, bf16[128,4096]{1,0:T(8,128)(2,1)} %bitcast.181, bf16[4096,128]{0,1:T(8,128)(2,1)S(1)} %copy-done.3, f32[4096]{0:T(1024)S(1)} %bitcast.199, bf16[3,64,4096]{2,1,0:T(8,128)(2,1)} %param.26, bf16[128,192]{0,1:T(8,128)(2,1)S(1)} %fusion.20), kind=kOutput, calls=%fused_computation.35 | convolution fusion | flops 205012992 | bytes 3735552 | tf_op jit(solution)/shard_map/while/body/eval_jaxpr/dot_general | solution.py:43
  103.1 4.7 %convolution_convert_fusion = bf16[128,512]{1,0:T(8,128)(2,1)S(1)} fusion(bf16[512,4096]{1,0:T(8,128)(2,1)} %param.31, bf16[128,4096]{1,0:T(8,128)(2,1)} %bitcast.182, bf16[4096,128]{0,1:T(8,128)(2,1)S(1)} %copy-done.3, f32[4096]{0:T(1024)S(1)} %bitcast.198, bf16[3,64,4096]{2,1,0:T(8,128)(2,1)} %param.26, bf16[128,192]{0,1:T(8,128)(2,1)S(1)} %fusion.20), kind=kOutput, calls=%fused_computation.29 | convolution fusion | flops 607715328 | bytes 6979584 | tf_op jit(solution)/shard_map/while/body/eval_jaxpr/dot_general | solution.py:51
  108.0 4.7 %fusion.19 = f32[128,512]{1,0:T(8,128)S(1)} fusion(bf16[512,4096]{1,0:T(8,128)(2,1)} %param.30, bf16[128,4096]{1,0:T(8,128)(2,1)} %bitcast.183, bf16[4096,128]{0,1:T(8,128)(2,1)S(1)} %copy-done.3, f32[4096]{0:T(1024)S(1)} %bitcast.197, bf16[3,64,4096]{2,1,0:T(8,128)(2,1)} %param.26, bf16[128,192]{0,1:T(8,128)(2,1)S(1)} %fusion.20), kind=kOutput, calls=%fused_computation.31 | convolution fusion | flops 607780864 | bytes 7110656 | tf_op jit(solution)/shard_map/while/body/eval_jaxpr/dot_general | solution.py:48
  112.8 3.3 %fusion.56 = f32[8,8,64,64]{3,2,1,0:T(8,128)} fusion(f32[8,16,8,64]{3,2,1,0:T(8,128)S(1)} %reshape.549, f32[8,16,8,64]{3,2,0,1:T(8,128)S(1)} %reduce_window_sum.15, bf16[8,16,8,64]{3,2,1,0:T(8,128)(2,1)S(1)} %reshape.535, f32[8,8,64]{2,1,0:T(8,128)S(1)} %sub.51, pred[8,16]{1,0:T(8,128)(4,1)S(1)} %copy.71), kind=kOutput, calls=%fused_computation.66 | convolution fusion | flops 50593792 | bytes 1720448 | tf_op jit(solution)/shard_map/while/body/eval_jaxpr/rlhi,rlhj->rhij/dot_general | solution.py:72
  116.1 2.9 %reshape_reshape.3 = f32[1,8,8,4096]{3,2,1,0:T(8,128)} reshape(f32[8,8,64,64]{3,2,1,0:T(8,128)} %fusion.56) | data formatting | bytes 2097152 | tf_op jit(solution)/shard_map/reshape;reshape | solution.py:193
  119.1 3.7 %all-to-all-start = ((f32[1,8,8,4096]{3,2,0,1:T(8,128)}), f32[1,8,8,4096]{3,2,0,1:T(8,128)S(1)}, u32[]{:S(2)}, u32[]{:S(2)}) async-start(f32[1,8,8,4096]{3,2,0,1:T(8,128)} %bitcast.13), calls=%async_computation | async-start | bytes 2097152 | tf_op jit(solution)/shard_map/all_to_all | solution.py:192
  123.6 23.9 %all-to-all-done = f32[1,8,8,4096]{3,2,0,1:T(8,128)S(1)} async-done(((f32[1,8,8,4096]{3,2,0,1:T(8,128)}), f32[1,8,8,4096]{3,2,0,1:T(8,128)S(1)}, u32[]{:S(2)}, u32[]{:S(2)}) %all-to-all-start) | async-done | bytes 1048608 | tf_op jit(solution)/shard_map/all_to_all | solution.py:192
  147.5 1.1 copy.77
  148.6 4.6 %all_to_all.21 = f32[1,1,64,4096]{3,1,0,2:T(1,128)S(1)} all-to-all(f32[1,1,64,4096]{3,1,0,2:T(1,128)S(1)} %copy.77), channel_id=1, replica_groups=mesh['groups'=2,'wide'=8,'narrow'=2] {'narrow'}, dimensions={2} | all-to-all | bytes 2097152 | tf_op jit(solution)/shard_map/all_to_all | solution.py:191
  153.1 2.6 %reduce.6 = f32[64,4096]{1,0:T(8,128)S(1)} reduce(f32[1,1,64,4096]{3,1,0,2:T(1,128)S(1)} %all_to_all.21, f32[]{:T(128)} %constant.68), dimensions={0,1}, to_apply=%all_to_all.8.reduce_sub_computation | reduce | bytes 2097156 | tf_op jit(solution)/shard_map/all_to_all | solution.py:191
  155.8 2.2 %reshape.536 = f32[2,32,64,64]{3,2,1,0:T(8,128)} reshape(f32[64,4096]{1,0:T(8,128)S(1)} %reduce.6) | data formatting | bytes 2097152 | tf_op jit(solution)/shard_map/reshape.34
  158.0 2.8 %fusion.99 = f32[2,32,1,64]{3,2,1,0:T(1,128)S(1)} fusion(f32[2,32,64,64]{3,2,1,0:T(8,128)} %reshape.536, bf16[2,32,64,1]{2,1,0,3:T(8,128)(2,1)S(1)} %get-tuple-element.61), kind=kOutput, calls=%fused_computation.127 | convolution fusion | flops 3145728 | bytes 1073152 | tf_op jit(solution)/shard_map/...hi,...hij->...hj/dot_general | solution.py:104
  160.8 2.0 %fusion.15 = f32[2,32,1,64]{3,2,1,0:T(1,128)S(1)} fusion(f32[2,32,64,64]{3,2,1,0:T(8,128)S(1)} %copy-done.2, f32[2,32,64]{2,1,0:T(8,128)S(1)} %get-tuple-element.70, f32[2,32,64]{2,1,0:T(8,128)S(1)} %get-tuple-element.54, f32[2,32,64]{2,1,0:T(8,128)S(1)} %get-tuple-element.37, bf16[2,32,64,1]{2,1,0,3:T(8,128)(2,1)S(1)} %get-tuple-element.64), kind=kOutput, calls=%fused_computation.23 | convolution fusion | flops 3932160 | bytes 1122304 | tf_op jit(solution)/shard_map/...hi,...hij->...hj/dot_general | solution.py:104
  162.8 3.5 %fusion.17 = f32[2,32,1,64]{3,2,1,0:T(1,128)S(1)} fusion(f32[2,32,64,64]{3,2,1,0:T(8,128)S(1)} %copy-done.2, f32[2,32,64]{2,1,0:T(8,128)S(1)} %get-tuple-element.68, f32[2,32,64]{2,1,0:T(8,128)S(1)} %get-tuple-element.56, f32[2,32,64]{2,1,0:T(8,128)S(1)} %get-tuple-element.52, f32[2,32,64]{2,1,0:T(8,128)S(1)} %get-tuple-element.70, ...), kind=kOutput, calls=%fused_computation.26 | convolution fusion | flops 4718592 | bytes 1171456 | tf_op jit(solution)/shard_map/...hi,...hij->...hj/dot_general | solution.py:104
  166.3 5.3 %fusion.11 = f32[2,32,1,64]{3,2,1,0:T(1,128)S(1)} fusion(f32[2,32,64,64]{3,2,1,0:T(8,128)S(1)} %copy-done.2, f32[2,32,64]{2,1,0:T(8,128)S(1)} %get-tuple-element.69, f32[2,32,64]{2,1,0:T(8,128)S(1)} %get-tuple-element.57, f32[2,32,64]{2,1,0:T(8,128)S(1)} %get-tuple-element.38, f32[2,32,64]{2,1,0:T(8,128)S(1)} %get-tuple-element.68, ...), kind=kOutput, calls=%fused_computation.17 | convolution fusion | flops 5505024 | bytes 1220608 | tf_op jit(solution)/shard_map/...hi,...hij->...hj/dot_general | solution.py:104
  173.0 0.7 fusion.81
  (77 shorter events, 3.3 us)
Async XLA Ops:
  6.5 92.3 %copy-start = (bf16[4096,192]{0,1:T(8,128)(2,1)S(1)}, bf16[4096,192]{0,1:T(8,128)(2,1)}, u32[]{:S(2)}) copy-start(bf16[4096,192]{0,1:T(8,128)(2,1)} %param.25) | copy-start | bytes 4718596
  6.5 90.7 %all-gather.2.cloned.1.call-start = ((), (), s32[]{:S(2)}) async-start(), calls=%async_computation.2 | async-start | bytes 1179648 | tf_op jit(solution)/shard_map/all_gather | solution.py:158
  8.2 46.8 %copy-start.14 = (s32[1,8]{1,0:T(1,128)S(1)}, s32[1,8]{1,0:T(1,128)}, u32[]{:S(2)}) copy-start(s32[1,8]{1,0:T(1,128)} %param.21) | copy-start | bytes 100
  8.2 46.9 %copy-start.6 = (f32[3,4096]{1,0:T(4,128)S(1)}, f32[3,4096]{1,0:T(4,128)}, u32[]{:S(2)}) copy-start(f32[3,4096]{1,0:T(4,128)} %param.24) | copy-start | bytes 147460
  52.2 46.6 %copy-start.15 = (f32[4096]{0:T(1024)S(1)}, f32[4096]{0:T(1024)}, u32[]{:S(2)}) copy-start(f32[4096]{0:T(1024)} %param.23) | copy-start | bytes 49156
  97.2 1.6 copy-start.3
  98.8 1.0 copy-start.4
  99.8 2.7 %copy-start.5 = (bf16[128,512]{1,0:T(8,128)(2,1)S(1)}, bf16[128,512]{1,0:T(8,128)(2,1)}, u32[]{:S(2)}) copy-start(bf16[128,512]{1,0:T(8,128)(2,1)} %param.29) | copy-start | bytes 393220
  99.8 2.7 %copy-start.13 = (f32[512]{0:T(512)S(1)}, f32[512]{0:T(512)}, u32[]{:S(2)}) copy-start(f32[512]{0:T(512)} %param.27) | copy-start | bytes 6148
  116.1 6.7 %copy-start.7 = (bf16[2,1,4,2048]{3,2,1,0:T(4,128)(2,1)S(1)}, bf16[2,1,4,2048]{3,2,1,0:T(4,128)(2,1)}, u32[]{:S(2)}) copy-start(bf16[2,1,4,2048]{3,2,1,0:T(4,128)(2,1)} %param.37) | copy-start | bytes 98308
  116.1 6.8 %copy-start.8 = (bf16[2,1,4,2048]{3,2,1,0:T(4,128)(2,1)S(1)}, bf16[2,1,4,2048]{3,2,1,0:T(4,128)(2,1)}, u32[]{:S(2)}) copy-start(bf16[2,1,4,2048]{3,2,1,0:T(4,128)(2,1)} %param.38) | copy-start | bytes 98308
  116.1 7.0 %copy-start.9 = (bf16[2,1,4,2048]{3,2,1,0:T(4,128)(2,1)S(1)}, bf16[2,1,4,2048]{3,2,1,0:T(4,128)(2,1)}, u32[]{:S(2)}) copy-start(bf16[2,1,4,2048]{3,2,1,0:T(4,128)(2,1)} %param.36) | copy-start | bytes 98308
  119.1 4.2 %copy-start.10 = (bf16[2,1,4,2048]{3,2,1,0:T(4,128)(2,1)S(1)}, bf16[2,1,4,2048]{3,2,1,0:T(4,128)(2,1)}, u32[]{:S(2)}) copy-start(bf16[2,1,4,2048]{3,2,1,0:T(4,128)(2,1)} %param.35) | copy-start | bytes 98308
  119.1 4.3 %copy-start.12 = (f32[64,64]{1,0:T(8,128)S(1)}, f32[64,64]{1,0:T(8,128)}, u32[]{:S(2)}) copy-start(f32[64,64]{1,0:T(8,128)} %param.32) | copy-start | bytes 49156
  119.1 28.4 %all-to-all-start = ((f32[1,8,8,4096]{3,2,0,1:T(8,128)}), f32[1,8,8,4096]{3,2,0,1:T(8,128)S(1)}, u32[]{:S(2)}, u32[]{:S(2)}) async-start(f32[1,8,8,4096]{3,2,0,1:T(8,128)} %bitcast.13), calls=%async_computation | async-start | bytes 2097152 | tf_op jit(solution)/shard_map/all_to_all | solution.py:192
  158.0 2.8 %copy-start.2 = (f32[2,32,64,64]{3,2,1,0:T(8,128)S(1)}, f32[2,32,64,64]{3,2,1,0:T(8,128)}, u32[]{:S(2)}) copy-start(f32[2,32,64,64]{3,2,1,0:T(8,128)} %reshape.536) | copy-start | bytes 3145732
  166.3 6.7 %copy-start.11 = (bf16[2,1,4,2048]{3,2,1,0:T(4,128)(2,1)S(1)}, bf16[2,1,4,2048]{3,2,1,0:T(4,128)(2,1)}, u32[]{:S(2)}) copy-start(bf16[2,1,4,2048]{3,2,1,0:T(4,128)(2,1)} %param.39) | copy-start | bytes 98308
  166.3 6.7 %dynamic-slice-start = ((f32[4096]{0:T(1024)}, s32[]{:T(128)}), f32[2048]{0:T(1024)S(1)}, s32[]{:S(2)}) async-start(f32[4096]{0:T(1024)} %param.33, s32[]{:T(128)} %select_n.43), calls=%async_computation.3 | async-start | bytes 16896 | tf_op jit(solution)/shard_map/dynamic_slice | solution.py:209
  166.3 6.6 %dynamic-slice-start.1 = ((f32[4096]{0:T(1024)}, s32[]{:T(128)}), f32[2048]{0:T(1024)S(1)}, s32[]{:S(2)}) async-start(f32[4096]{0:T(1024)} %param.34, s32[]{:T(128)} %select_n.43), calls=%async_computation.4 | async-start | bytes 16896 | tf_op jit(solution)/shard_map/dynamic_slice | solution.py:215
  166.3 7.4 %copy-start.1 = (bf16[4096,192]{0,1:T(8,128)(2,1)S(1)}, bf16[4096,192]{0,1:T(8,128)(2,1)}, u32[]{:S(2)}) copy-start(bf16[4096,192]{0,1:T(8,128)(2,1)} %param.25) | copy-start | bytes 4718596
Sparse Core Ops, SparseCore 0:
  55.1 42.1 all-gather.1
where the time goes:
time: 182 us; the launch traced here: 181 us
  waiting for transfers between devices  66 us (36%)
  local copies, waits for them, and re-layouts  57.7 us (32%)
  matrix products  29.8 us (16%)
  between operations  13.8 us (8%)
  other arithmetic  4.89 us (3%)
  blocking collectives  4.58 us (3%)
  starting transfers between devices  3.75 us (2%)
    unnamed x33, local copies, waits for them, and re-layouts  44.4 us
    all_gather x1, waiting for transfers between devices, per_device(): gathered = lax.all_gather(picked, 'wide', axis=0, tiled=True).T  42.1 us
    all_to_all x1, waiting for transfers between devices, per_device(): lax.all_to_all(recurrent_memories.reshape(1, bank_rows, head_local, atten...  23.9 us
    dot_general x4, matrix products, generation_iterations(): jnp.einsum('...hi,...hij->...hj', present_acceptance, recurrent_memories,...  13.7 us
    dot_general x1, matrix products, mix_project(): jnp.dot(branches[1], address_projector.T, preferred_element_type=jnp.floa...  4.66 us
    dot_general x1, matrix products, mix_project(): jnp.dot(branches[2], payload_projector.T, preferred_element_type=jnp.floa...  4.66 us
    all_to_all x1, blocking collectives, per_device(): lax.all_to_all(lax.all_to_all(recurrent_memories.reshape(1, bank_rows, he...  4.58 us
    all_to_all x1, starting transfers between devices, per_device(): lax.all_to_all(recurrent_memories.reshape(1, bank_rows, head_local, atten...  3.75 us
  transfers between devices with their start and end apart: 2, of which 2 were waited for; matrix products, arithmetic and copies ran while one was open for 0% of the time, Pallas kernels for 0%

commit v1 on v0

--- a/solution.py
+++ b/solution.py
@@ -189,12 +189,22 @@
         bank_rows, head_local, attender_width, attender_width
     )
     handed = lax.all_to_all(
-        lax.all_to_all(
-            recurrent_memories.reshape(1, bank_rows, head_local, attender_width * attender_width),
-            "wide",
-            split_axis=1,
-            concat_axis=2,
-            tiled=True,
+        jnp.concatenate(
+            lax.all_to_all(
+                jnp.stack(
+                    jnp.split(
+                        recurrent_memories.reshape(
+                            1, bank_rows, head_local, attender_width * attender_width
+                        ),
+                        lax.axis_size("wide"),
+                        axis=1,
+                    )
+                ),
+                "wide",
+                0,
+                0,
+            ),
+            axis=2,
         ),
         "narrow",
         split_axis=2,

time: 182 us -> 189 us (1.038)
  local copies, waits for them, and re-layouts: 57.7 us -> 63.3 us
    unnamed x33 -> x40, local copies, waits for them, and re-layouts: 44.4 us -> 49 us
    reshape x0 -> x1, local copies, waits for them, and re-layouts: none -> 2.21 us  [per_device(): jnp.concatenate(lax.all_to_all(jnp.stack(jnp.split(recurrent_memories.res...]
where the time goes in v1:
time: 189 us; the launch traced here: 187 us
  waiting for transfers between devices  66 us (35%)
  local copies, waits for them, and re-layouts  63.3 us (33%)
  matrix products  29.8 us (16%)
  between operations  13.8 us (7%)
  blocking collectives  5.68 us (3%)
  other arithmetic  4.89 us (3%)
  starting transfers between devices  3.62 us (2%)
    unnamed x40, local copies, waits for them, and re-layouts  49 us
    all_gather x1, waiting for transfers between devices, per_device(): gathered = lax.all_gather(picked, 'wide', axis=0, tiled=True).T  42.1 us
    all_to_all x1, waiting for transfers between devices, per_device(): lax.all_to_all(jnp.stack(jnp.split(recurrent_memories.reshape(1, bank_row...  23.9 us
    dot_general x4, matrix products, generation_iterations(): jnp.einsum('...hi,...hij->...hj', present_acceptance, recurrent_memories,...  13.7 us
    all_to_all x1, blocking collectives, per_device(): lax.all_to_all(jnp.concatenate(lax.all_to_all(jnp.stack(jnp.split(recurre...  5.68 us
    dot_general x1, matrix products, mix_project(): jnp.dot(branches[1], address_projector.T, preferred_element_type=jnp.floa...  4.66 us
    dot_general x1, matrix products, mix_project(): jnp.dot(branches[2], payload_projector.T, preferred_element_type=jnp.floa...  4.66 us
  transfers between devices with their start and end apart: 2, of which 2 were waited for; matrix products, arithmetic and copies ran while one was open for 0% of the time, Pallas kernels for 0%

profile of v1, /device:TPU:0, one launch (start us, length us, event | category | flops | bytes accessed | tf_op | source)
XLA Modules:
  0.0 187.2 jit_solution(10193676445742396559)
XLA Ops:
  6.5 0.9 reshape.534
  7.4 0.8 reshape.533
  8.2 44.0 %copy.68 = bf16[512,32768]{0,1:T(8,128)(2,1)} copy(bf16[512,32768]{1,0:T(8,128)(2,1)} %param.22) | data formatting | bytes 67108864 | tf_op args[2]
  52.2 2.0 %gather_fusion = bf16[128,512]{1,0:T(8,128)(2,1)S(1)} fusion(bf16[512,32768]{0,1:T(8,128)(2,1)} %copy.68, s32[1024]{0:T(1024)S(1)} %pad_clamp_fusion), kind=kCustom, calls=%fused_computation | custom fusion | bytes 262656 | tf_op jit(solution)/shard_map/jit(_take)/gather | solution.py:157
  54.2 0.7 select_bitcast_fusion
  55.1 42.1 %all-gather.2.cloned.1.call-done = bf16[4096,128]{0,1:T(8,128)(2,1)} async-done(((bf16[512,128]{0,1:T(8,128)(2,1)}), bf16[4096,128]{0,1:T(8,128)(2,1)}) %all-gather.2.cloned.1.call-update) | async-done | bytes 1048592 | tf_op jit(solution)/shard_map/all_gather | solution.py:158
  97.2 1.6 pad_slice_fusion
  98.8 0.7 fusion.20
  99.8 2.7 %fusion.22 = bf16[128,128]{1,0:T(8,128)(2,1)S(1)} fusion(bf16[4096,128]{1,0:T(8,128)(2,1)} %param.28, bf16[128,4096]{1,0:T(8,128)(2,1)} %bitcast.212, bf16[4096,128]{0,1:T(8,128)(2,1)S(1)} %copy-done.3, f32[4096]{0:T(1024)S(1)} %bitcast.230, bf16[3,64,4096]{2,1,0:T(8,128)(2,1)} %param.26, bf16[128,192]{0,1:T(8,128)(2,1)S(1)} %fusion.20), kind=kOutput, calls=%fused_computation.35 | convolution fusion | flops 205012992 | bytes 3735552 | tf_op jit(solution)/shard_map/while/body/eval_jaxpr/dot_general | solution.py:43
  103.1 4.7 %convolution_convert_fusion = bf16[128,512]{1,0:T(8,128)(2,1)S(1)} fusion(bf16[512,4096]{1,0:T(8,128)(2,1)} %param.31, bf16[128,4096]{1,0:T(8,128)(2,1)} %bitcast.213, bf16[4096,128]{0,1:T(8,128)(2,1)S(1)} %copy-done.3, f32[4096]{0:T(1024)S(1)} %bitcast.229, bf16[3,64,4096]{2,1,0:T(8,128)(2,1)} %param.26, bf16[128,192]{0,1:T(8,128)(2,1)S(1)} %fusion.20), kind=kOutput, calls=%fused_computation.29 | convolution fusion | flops 607715328 | bytes 6979584 | tf_op jit(solution)/shard_map/while/body/eval_jaxpr/dot_general | solution.py:51
  108.0 4.7 %fusion.19 = f32[128,512]{1,0:T(8,128)S(1)} fusion(bf16[512,4096]{1,0:T(8,128)(2,1)} %param.30, bf16[128,4096]{1,0:T(8,128)(2,1)} %bitcast.214, bf16[4096,128]{0,1:T(8,128)(2,1)S(1)} %copy-done.3, f32[4096]{0:T(1024)S(1)} %bitcast.228, bf16[3,64,4096]{2,1,0:T(8,128)(2,1)} %param.26, bf16[128,192]{0,1:T(8,128)(2,1)S(1)} %fusion.20), kind=kOutput, calls=%fused_computation.31 | convolution fusion | flops 607780864 | bytes 7110656 | tf_op jit(solution)/shard_map/while/body/eval_jaxpr/dot_general | solution.py:48
  112.8 3.3 %fusion.56 = f32[8,8,64,64]{3,2,1,0:T(8,128)} fusion(f32[8,16,8,64]{3,2,1,0:T(8,128)S(1)} %reshape.550, f32[8,16,8,64]{3,2,0,1:T(8,128)S(1)} %reduce_window_sum.15, bf16[8,16,8,64]{3,2,1,0:T(8,128)(2,1)S(1)} %reshape.535, f32[8,8,64]{2,1,0:T(8,128)S(1)} %sub.51, pred[8,16]{1,0:T(8,128)(4,1)S(1)} %copy.69), kind=kOutput, calls=%fused_computation.66 | convolution fusion | flops 50593792 | bytes 1720448 | tf_op jit(solution)/shard_map/while/body/eval_jaxpr/rlhi,rlhj->rhij/dot_general | solution.py:72
  116.1 2.1 %reshape_reshape.3 = f32[1,8,8,4096]{3,2,1,0:T(8,128)S(1)} reshape(f32[8,8,64,64]{3,2,1,0:T(8,128)} %fusion.56) | data formatting | bytes 2097152 | tf_op jit(solution)/shard_map/reshape;reshape | solution.py:196
  123.6 3.6 %all-to-all-start = ((f32[8,1,1,8,4096]{4,3,2,1,0:T(8,128)}), f32[8,1,1,8,4096]{4,3,2,1,0:T(8,128)S(1)}, u32[]{:S(2)}, u32[]{:S(2)}) async-start(f32[8,1,1,8,4096]{4,3,2,1,0:T(8,128)} %fusion.72), calls=%async_computation | async-start | bytes 2097152 | tf_op jit(solution)/shard_map/all_to_all | solution.py:193
  127.9 23.9 %all-to-all-done = f32[8,1,1,8,4096]{4,3,2,1,0:T(8,128)S(1)} async-done(((f32[8,1,1,8,4096]{4,3,2,1,0:T(8,128)}), f32[8,1,1,8,4096]{4,3,2,1,0:T(8,128)S(1)}, u32[]{:S(2)}, u32[]{:S(2)}) %all-to-all-start) | async-done | bytes 1048608 | tf_op jit(solution)/shard_map/all_to_all | solution.py:193
  151.9 2.2 %reshape.536 = f32[1,1,64,4096]{3,1,0,2:T(1,128)} reshape(f32[8,1,1,8,4096]{4,3,2,1,0:T(8,128)S(1)} %all-to-all-done) | data formatting | bytes 2097152 | tf_op jit(solution)/shard_map/reshape | solution.py:192
  154.1 5.7 %all_to_all.14 = f32[1,1,64,4096]{3,1,0,2:T(1,128)S(1)} all-to-all(f32[1,1,64,4096]{3,1,0,2:T(1,128)} %reshape.536), channel_id=1, replica_groups=mesh['groups'=2,'wide'=8,'narrow'=2] {'narrow'}, dimensions={2} | all-to-all | bytes 2097152 | tf_op jit(solution)/shard_map/all_to_all | solution.py:191
  159.8 2.6 %reduce.6 = f32[64,4096]{1,0:T(8,128)S(1)} reduce(f32[1,1,64,4096]{3,1,0,2:T(1,128)S(1)} %all_to_all.14, f32[]{:T(128)} %constant.68), dimensions={0,1}, to_apply=%all_to_all.5.reduce_sub_computation | reduce | bytes 2097156 | tf_op jit(solution)/shard_map/all_to_all | solution.py:191
  162.4 2.2 %reshape.537 = f32[2,32,64,64]{3,2,1,0:T(8,128)} reshape(f32[64,4096]{1,0:T(8,128)S(1)} %reduce.6) | data formatting | bytes 2097152 | tf_op jit(solution)/shard_map/reshape.33
  164.6 2.8 %fusion.107 = f32[2,32,1,64]{3,2,1,0:T(1,128)S(1)} fusion(f32[2,32,64,64]{3,2,1,0:T(8,128)} %reshape.537, bf16[2,32,64,1]{2,1,0,3:T(8,128)(2,1)S(1)} %get-tuple-element.61), kind=kOutput, calls=%fused_computation.143 | convolution fusion | flops 3145728 | bytes 1073152 | tf_op jit(solution)/shard_map/...hi,...hij->...hj/dot_general | solution.py:104
  167.4 2.0 %fusion.15 = f32[2,32,1,64]{3,2,1,0:T(1,128)S(1)} fusion(f32[2,32,64,64]{3,2,1,0:T(8,128)S(1)} %copy-done.2, f32[2,32,64]{2,1,0:T(8,128)S(1)} %get-tuple-element.70, f32[2,32,64]{2,1,0:T(8,128)S(1)} %get-tuple-element.54, f32[2,32,64]{2,1,0:T(8,128)S(1)} %get-tuple-element.37, bf16[2,32,64,1]{2,1,0,3:T(8,128)(2,1)S(1)} %get-tuple-element.64), kind=kOutput, calls=%fused_computation.23 | convolution fusion | flops 3932160 | bytes 1122304 | tf_op jit(solution)/shard_map/...hi,...hij->...hj/dot_general | solution.py:104
  169.4 3.5 %fusion.17 = f32[2,32,1,64]{3,2,1,0:T(1,128)S(1)} fusion(f32[2,32,64,64]{3,2,1,0:T(8,128)S(1)} %copy-done.2, f32[2,32,64]{2,1,0:T(8,128)S(1)} %get-tuple-element.68, f32[2,32,64]{2,1,0:T(8,128)S(1)} %get-tuple-element.56, f32[2,32,64]{2,1,0:T(8,128)S(1)} %get-tuple-element.52, f32[2,32,64]{2,1,0:T(8,128)S(1)} %get-tuple-element.70, ...), kind=kOutput, calls=%fused_computation.26 | convolution fusion | flops 4718592 | bytes 1171456 | tf_op jit(solution)/shard_map/...hi,...hij->...hj/dot_general | solution.py:104
  172.9 5.3 %fusion.11 = f32[2,32,1,64]{3,2,1,0:T(1,128)S(1)} fusion(f32[2,32,64,64]{3,2,1,0:T(8,128)S(1)} %copy-done.2, f32[2,32,64]{2,1,0:T(8,128)S(1)} %get-tuple-element.69, f32[2,32,64]{2,1,0:T(8,128)S(1)} %get-tuple-element.57, f32[2,32,64]{2,1,0:T(8,128)S(1)} %get-tuple-element.38, f32[2,32,64]{2,1,0:T(8,128)S(1)} %get-tuple-element.68, ...), kind=kOutput, calls=%fused_computation.17 | convolution fusion | flops 5505024 | bytes 1220608 | tf_op jit(solution)/shard_map/...hi,...hij->...hj/dot_general | solution.py:104
  179.6 0.7 fusion.89
  (85 shorter events, 8.6 us)
Async XLA Ops:
  6.5 92.3 %copy-start = (bf16[4096,192]{0,1:T(8,128)(2,1)S(1)}, bf16[4096,192]{0,1:T(8,128)(2,1)}, u32[]{:S(2)}) copy-start(bf16[4096,192]{0,1:T(8,128)(2,1)} %param.25) | copy-start | bytes 4718596
  6.5 90.7 %all-gather.2.cloned.1.call-start = ((), (), s32[]{:S(2)}) async-start(), calls=%async_computation.2 | async-start | bytes 1179648 | tf_op jit(solution)/shard_map/all_gather | solution.py:158
  8.2 46.8 %copy-start.14 = (s32[1,8]{1,0:T(1,128)S(1)}, s32[1,8]{1,0:T(1,128)}, u32[]{:S(2)}) copy-start(s32[1,8]{1,0:T(1,128)} %param.21) | copy-start | bytes 100
  8.2 46.9 %copy-start.6 = (f32[3,4096]{1,0:T(4,128)S(1)}, f32[3,4096]{1,0:T(4,128)}, u32[]{:S(2)}) copy-start(f32[3,4096]{1,0:T(4,128)} %param.24) | copy-start | bytes 147460
  52.2 46.6 %copy-start.15 = (f32[4096]{0:T(1024)S(1)}, f32[4096]{0:T(1024)}, u32[]{:S(2)}) copy-start(f32[4096]{0:T(1024)} %param.23) | copy-start | bytes 49156
  97.2 1.6 copy-start.3
  98.8 1.0 copy-start.4
  99.8 2.7 %copy-start.5 = (bf16[128,512]{1,0:T(8,128)(2,1)S(1)}, bf16[128,512]{1,0:T(8,128)(2,1)}, u32[]{:S(2)}) copy-start(bf16[128,512]{1,0:T(8,128)(2,1)} %param.29) | copy-start | bytes 393220
  99.8 2.7 %copy-start.13 = (f32[512]{0:T(512)S(1)}, f32[512]{0:T(512)}, u32[]{:S(2)}) copy-start(f32[512]{0:T(512)} %param.27) | copy-start | bytes 6148
  118.3 8.9 %copy-start.7 = (bf16[2,1,4,2048]{3,2,1,0:T(4,128)(2,1)S(1)}, bf16[2,1,4,2048]{3,2,1,0:T(4,128)(2,1)}, u32[]{:S(2)}) copy-start(bf16[2,1,4,2048]{3,2,1,0:T(4,128)(2,1)} %param.37) | copy-start | bytes 98308
  118.9 8.4 %copy-start.8 = (bf16[2,1,4,2048]{3,2,1,0:T(4,128)(2,1)S(1)}, bf16[2,1,4,2048]{3,2,1,0:T(4,128)(2,1)}, u32[]{:S(2)}) copy-start(bf16[2,1,4,2048]{3,2,1,0:T(4,128)(2,1)} %param.38) | copy-start | bytes 98308
  119.6 7.9 %copy-start.9 = (bf16[2,1,4,2048]{3,2,1,0:T(4,128)(2,1)S(1)}, bf16[2,1,4,2048]{3,2,1,0:T(4,128)(2,1)}, u32[]{:S(2)}) copy-start(bf16[2,1,4,2048]{3,2,1,0:T(4,128)(2,1)} %param.36) | copy-start | bytes 98308
  119.6 8.0 %copy-start.10 = (bf16[2,1,4,2048]{3,2,1,0:T(4,128)(2,1)S(1)}, bf16[2,1,4,2048]{3,2,1,0:T(4,128)(2,1)}, u32[]{:S(2)}) copy-start(bf16[2,1,4,2048]{3,2,1,0:T(4,128)(2,1)} %param.35) | copy-start | bytes 98308
  120.3 7.4 %copy-start.12 = (f32[64,64]{1,0:T(8,128)S(1)}, f32[64,64]{1,0:T(8,128)}, u32[]{:S(2)}) copy-start(f32[64,64]{1,0:T(8,128)} %param.32) | copy-start | bytes 49156
  123.6 28.3 %all-to-all-start = ((f32[8,1,1,8,4096]{4,3,2,1,0:T(8,128)}), f32[8,1,1,8,4096]{4,3,2,1,0:T(8,128)S(1)}, u32[]{:S(2)}, u32[]{:S(2)}) async-start(f32[8,1,1,8,4096]{4,3,2,1,0:T(8,128)} %fusion.72), calls=%async_computation | async-start | bytes 2097152 | tf_op jit(solution)/shard_map/all_to_all | solution.py:193
  164.6 2.8 %copy-start.2 = (f32[2,32,64,64]{3,2,1,0:T(8,128)S(1)}, f32[2,32,64,64]{3,2,1,0:T(8,128)}, u32[]{:S(2)}) copy-start(f32[2,32,64,64]{3,2,1,0:T(8,128)} %reshape.537) | copy-start | bytes 3145732
  172.9 6.7 %copy-start.11 = (bf16[2,1,4,2048]{3,2,1,0:T(4,128)(2,1)S(1)}, bf16[2,1,4,2048]{3,2,1,0:T(4,128)(2,1)}, u32[]{:S(2)}) copy-start(bf16[2,1,4,2048]{3,2,1,0:T(4,128)(2,1)} %param.39) | copy-start | bytes 98308
  172.9 6.7 %dynamic-slice-start = ((f32[4096]{0:T(1024)}, s32[]{:T(128)}), f32[2048]{0:T(1024)S(1)}, s32[]{:S(2)}) async-start(f32[4096]{0:T(1024)} %param.33, s32[]{:T(128)} %select_n.43), calls=%async_computation.3 | async-start | bytes 16896 | tf_op jit(solution)/shard_map/dynamic_slice | solution.py:219
  172.9 6.6 %dynamic-slice-start.1 = ((f32[4096]{0:T(1024)}, s32[]{:T(128)}), f32[2048]{0:T(1024)S(1)}, s32[]{:S(2)}) async-start(f32[4096]{0:T(1024)} %param.34, s32[]{:T(128)} %select_n.43), calls=%async_computation.4 | async-start | bytes 16896 | tf_op jit(solution)/shard_map/dynamic_slice | solution.py:225
  172.9 7.4 %copy-start.1 = (bf16[4096,192]{0,1:T(8,128)(2,1)S(1)}, bf16[4096,192]{0,1:T(8,128)(2,1)}, u32[]{:S(2)}) copy-start(bf16[4096,192]{0,1:T(8,128)(2,1)} %param.25) | copy-start | bytes 4718596
Sparse Core Ops, SparseCore 0:
  55.1 42.1 all-gather.1
